TPU v7x, 128 devices: a whole 4x4x4 slice. The times are simulated.
128 devices in a mesh: section: 8 (over z_lo, y), dp: 16 (over z_hi, x, core).
Axes of the slice: x: 4, y: 4, z: 4 (z_hi: 2, z_lo: 2; z = z_hi * 2 + z_lo), core: 2. Of those that a mesh axis runs over, the one named last changes fastest.
Arguments:
- enc_in: bfloat16 [8, 2, 8192, 1152], P('section', None, 'dp'), may hold values from -6 to 6
- dec_in: bfloat16 [8, 2, 8192, 1152], P('section', None, 'dp'), may hold values from -6 to 6
- cotangent: bfloat16 [8, 2, 8192, 1152], P('section', None, 'dp'), may hold values from -0.23925781 to 0.23925781
- w_proj: float32 [8, 1152, 1152], P('section', 'dp'), may hold values from -0.1875 to 0.1875
- w_skip: float32 [8, 2304, 1152], P('section', 'dp'), may hold values from -0.125 to 0.125
- m_proj: float32 [8, 1152, 1152], P('section', 'dp'), may hold values from -3 to 3
- v_proj: float32 [8, 1152, 1152], P('section', 'dp'), may hold values from 0.05 to 1
- m_skip: float32 [8, 2304, 1152], P('section', 'dp'), may hold values from -3 to 3
- v_skip: float32 [8, 2304, 1152], P('section', 'dp'), may hold values from 0.05 to 1
Outputs:
- dec_out: bfloat16 [8, 2, 8192, 1152], P('section', None, 'dp')
- enc_grad: bfloat16 [8, 2, 8192, 1152], P('section', None, 'dp')
- dec_grad: bfloat16 [8, 2, 8192, 1152], P('section', None, 'dp')
- new_w_proj: float32 [8, 1152, 1152], P('section', 'dp')
- new_m_proj: float32 [8, 1152, 1152], P('section', 'dp')
- new_v_proj: float32 [8, 1152, 1152], P('section', 'dp')
- new_w_skip: float32 [8, 2304, 1152], P('section', 'dp')
- new_m_skip: float32 [8, 2304, 1152], P('section', 'dp')
- new_v_skip: float32 [8, 2304, 1152], P('section', 'dp')
All inputs are finite; a program needn't handle non-finite values.
Results may differ from a plain program's by a relative error of at most 0.025.
Values may be sent and summed in bfloat16 or wider, within the bound.
A program may use at most 128 MiB of HBM per device.

v0:
```python
import jax
import jax.numpy as jnp
from jax import lax
from jax.sharding import PartitionSpec as P

half_root = 0.7071067811865476
gauss_norm = 0.3989422804014327
beta_one = 0.9
beta_two = 0.95
learn_rate = 0.002
adam_eps = 1e-08
correct_one = 1.0 - 0.9**10
correct_two = 1.0 - 0.95**10


def swapped(value, axis, bit):
    mask = 2**bit
    pairs = [(source, source ^ mask) for source in range(lax.axis_size(axis))]
    return lax.ppermute(value, axis, pairs)


def in_blocks(value, dim, count):
    before, after = (value.shape[:dim], value.shape[dim + 1 :])
    return jnp.moveaxis(value.reshape(*before, count, -1, *after), dim, 0)


def one_scatter(arrays, axis, dims):
    count = lax.axis_size(axis)
    pieces = [in_blocks(a, dim, count) for a, dim in zip(arrays, dims)]
    lines = jnp.concatenate([b.reshape(count, -1) for b in pieces], axis=1)
    span = max(16, -(-lines.shape[1] // 1024) * 8)
    lines = jnp.pad(lines, ((0, 0), (0, span * 128 - lines.shape[1]))).reshape(-1, 128)
    ravelled, at, outs = (lax.psum_scatter(lines, axis, tiled=True).reshape(-1), 0, [])
    for b in pieces:
        part = b[0]
        outs.append(ravelled[at : at + part.size].reshape(part.shape))
        at += part.size
    return tuple(outs)


def gelu_parts(preact):
    normal_cdf = 0.5 * (1.0 + lax.erf(preact * half_root))
    density = jnp.exp(-0.5 * preact * preact) * gauss_norm
    return (preact * normal_cdf, normal_cdf + preact * density)


def adam_update(weight, moment, second, grad):
    new_moment = beta_one * moment + (1.0 - beta_one) * grad
    new_second = beta_two * second + (1.0 - beta_two) * grad * grad
    step_size = new_moment / correct_one / (jnp.sqrt(new_second / correct_two) + adam_eps)
    return (weight - learn_rate * step_size, new_moment, new_second)


def top_bit():
    return lax.axis_size("section").bit_length() - 2


def send_forward(value):
    return swapped(value, "section", top_bit())


def send_backward(value):
    return swapped(value, "section", top_bit())


def layer_pass(enc_rows, dec_rows, out_grad, proj_full, skip_full):
    width = enc_rows.shape[1]
    skip_local = jnp.dot(enc_rows, proj_full, preferred_element_type=jnp.float32).astype(
        jnp.bfloat16
    )
    skip_remote = send_forward(skip_local)
    joined = jnp.concatenate([dec_rows, skip_remote], axis=1)
    preact = jnp.dot(joined, skip_full, preferred_element_type=jnp.float32)
    activated, gelu_slope = gelu_parts(preact)
    dec_out = activated.astype(jnp.bfloat16)
    pre_grad = (out_grad.astype(jnp.float32) * gelu_slope).astype(jnp.bfloat16)
    input_grad = jnp.einsum("rk,jk->rj", pre_grad, skip_full, preferred_element_type=jnp.float32)
    dec_grad = input_grad[:, :width].astype(jnp.bfloat16)
    skip_sent = input_grad[:, width:].astype(jnp.bfloat16)
    skip_grad = send_backward(skip_sent)
    enc_grad = jnp.einsum(
        "rk,jk->rj", skip_grad, proj_full, preferred_element_type=jnp.float32
    ).astype(jnp.bfloat16)
    grad_proj = jnp.einsum("rj,rk->jk", enc_rows, skip_grad, preferred_element_type=jnp.float32)
    grad_skip = jnp.einsum("rj,rk->jk", joined, pre_grad, preferred_element_type=jnp.float32)
    return (dec_out, enc_grad, dec_grad, grad_proj, grad_skip)


def body(enc_in, dec_in, cotangent, w_proj, w_skip, m_proj, v_proj, m_skip, v_skip):
    proj_all, skip_all = (
        lax.all_gather(w_proj.astype(jnp.bfloat16), "dp", axis=1, tiled=True),
        lax.all_gather(w_skip.astype(jnp.bfloat16), "dp", axis=1, tiled=True),
    )
    proj_full = proj_all[0]
    skip_full = skip_all[0]
    micro = enc_in.shape[1]
    tokens_here = enc_in.shape[2]
    width = enc_in.shape[3]
    rows = micro * tokens_here
    result = layer_pass(
        enc_in[0].reshape(rows, width),
        dec_in[0].reshape(rows, width),
        cotangent[0].reshape(rows, width),
        proj_full,
        skip_full,
    )
    dec_out = result[0].reshape(micro, tokens_here, width)
    enc_grad = result[1].reshape(micro, tokens_here, width)
    dec_grad = result[2].reshape(micro, tokens_here, width)
    proj_sum, skip_sum = tuple(
        (
            part.astype(jnp.float32)
            for part in one_scatter(
                (result[3].astype(jnp.bfloat16), result[4].astype(jnp.bfloat16)), "dp", (0, 0)
            )
        )
    )
    new_w_proj, new_m_proj, new_v_proj = adam_update(w_proj[0], m_proj[0], v_proj[0], proj_sum)
    new_w_skip, new_m_skip, new_v_skip = adam_update(w_skip[0], m_skip[0], v_skip[0], skip_sum)
    return (
        dec_out[None],
        enc_grad[None],
        dec_grad[None],
        new_w_proj[None],
        new_m_proj[None],
        new_v_proj[None],
        new_w_skip[None],
        new_m_skip[None],
        new_v_skip[None],
    )


def solution(mesh):
    in_specs = (
        P("section", None, "dp", None),
        P("section", None, "dp", None),
        P("section", None, "dp", None),
        P("section", "dp", None),
        P("section", "dp", None),
        P("section", "dp", None),
        P("section", "dp", None),
        P("section", "dp", None),
        P("section", "dp", None),
    )
    out_specs = (
        P("section", None, "dp", None),
        P("section", None, "dp", None),
        P("section", None, "dp", None),
        P("section", "dp", None),
        P("section", "dp", None),
        P("section", "dp", None),
        P("section", "dp", None),
        P("section", "dp", None),
        P("section", "dp", None),
    )
    return jax.shard_map(body, mesh=mesh, in_specs=in_specs, out_specs=out_specs, check_vma=False)
```

profile of v0, /device:TPU:0, one launch (start us, length us, event | category | flops | bytes accessed | tf_op | source)
XLA Modules:
  0.0 429.5 jit_solution(92079628465543061)
XLA Ops:
  7.2 0.0 copy-start
  7.2 0.0 all-gather.3.cloned.1.call-start
  7.2 1.8 convert_element_type.71
  9.0 0.0 all-gather.3.cloned.1.call-update
  9.1 0.0 all-gather.5.cloned.1.call-start
  9.1 1.9 convert_element_type.73
  11.0 0.0 all-gather.5.cloned.1.call-update
  11.0 0.0 all-reduce.3.cloned.1.call-start
  11.1 52.7 %all-gather.3.cloned.1.call-done = bf16[1,1152,1152]{2,1,0:T(8,128)(2,1)} async-done(((bf16[1,72,1152]{2,1,0:T(8,128)(2,1)}), bf16[1,1152,1152]{2,1,0:T(8,128)(2,1)}) %all-gather.3.cloned.1.call-update) | async-done | bytes 2654224 | tf_op jit(solution)/shard_map/all_gather | solution.py:91
  63.7 0.0 copy-done
  63.7 5.4 %convolution_convert_fusion.4 = bf16[1024,1152]{1,0:T(8,128)(2,1)S(1)} fusion(bf16[1024,1152]{1,0:T(8,128)(2,1)S(1)} %bitcast.29, bf16[1,1152,1152]{2,1,0:T(8,128)(2,1)} %all-gather.3.cloned.1.call-done), kind=kOutput, calls=%fused_computation.19 | convolution fusion | flops 2719088640 | bytes 7372800 | tf_op jit(solution)/shard_map/dot_general | solution.py:68
  69.2 0.7 collective-permute-start
  69.9 70.6 %collective-permute-done = bf16[1024,1152]{1,0:T(8,128)(2,1)} collective-permute-done((bf16[1024,1152]{1,0:T(8,128)(2,1)S(1)}, bf16[1024,1152]{1,0:T(8,128)(2,1)}, u32[]{:S(2)}, u32[]{:S(2)}) %collective-permute-start) | collective-permute-done | bytes 2359328 | tf_op jit(solution)/shard_map/ppermute | solution.py:19
  140.5 1.6 all-gather.5.cloned.1.call-done
  142.1 0.0 copy-start.3
  142.1 13.2 %fusion.9 = (bf16[1024,1152]{1,0:T(8,128)(2,1)S(1)}, bf16[1024,1152]{1,0:T(8,128)(2,1)}) fusion(bf16[1,2,512,1152]{3,2,1,0:T(8,128)(2,1)} %param.11, bf16[1,2304,1152]{2,1,0:T(8,128)(2,1)} %all-gather.5.cloned.1.call-done, bf16[1024,1152]{1,0:T(8,128)(2,1)} %collective-permute-done, bf16[1024,1152]{1,0:T(8,128)(2,1)} %bitcast.32), kind=kOutput, calls=%fused_computation.14 | convolution fusion | flops 5460590592 | bytes 17104896 | tf_op jit(solution)/shard_map/dot_general | solution.py:73
  155.3 0.0 copy-done.3
  155.3 6.5 %convolution_convert_fusion.2 = bf16[1024,2304]{1,0:T(8,128)(2,1)S(1)} fusion(bf16[1024,1152]{1,0:T(8,128)(2,1)S(1)} %get-tuple-element.17, bf16[1,2304,1152]{2,1,0:T(8,128)(2,1)S(1)} %copy-done.3), kind=kOutput, calls=%fused_computation.5 | convolution fusion | flops 5438177280 | bytes 12386304 | tf_op jit(solution)/shard_map/rk,jk->rj/dot_general | solution.py:77
  161.9 0.0 copy-start.4
  161.9 2.5 fusion.18
  164.4 0.7 collective-permute-start.1
  165.1 0.0 copy-done.4
  165.1 8.4 %convolution_convert_fusion = bf16[2304,1152]{1,0:T(8,128)(2,1)} fusion(bf16[1024,1152]{1,0:T(8,128)(2,1)S(1)} %get-tuple-element.17, bf16[1024,1152]{1,0:T(8,128)(2,1)} %collective-permute-done, bf16[1024,1152]{1,0:T(8,128)(2,1)S(1)} %bitcast.33), kind=kOutput, calls=%fused_computation | convolution fusion | flops 5447909376 | bytes 12386304 | tf_op jit(solution)/shard_map/rj,rk->jk/dot_general | solution.py:85
  173.5 5.7 %reshape_reshape.7 = bf16[16,165888]{1,0:T(8,128)(2,1)} reshape(bf16[2304,1152]{1,0:T(8,128)(2,1)} %convolution_convert_fusion) | data formatting | bytes 10616832 | tf_op jit(solution)/shard_map/reshape;reshape | solution.py:30
  179.2 39.0 %collective-permute-done.1 = bf16[1024,1152]{1,0:T(8,128)(2,1)} collective-permute-done((bf16[1024,1152]{1,0:T(8,128)(2,1)}, bf16[1024,1152]{1,0:T(8,128)(2,1)}, u32[]{:S(2)}, u32[]{:S(2)}) %collective-permute-start.1) | collective-permute-done | bytes 2359328 | tf_op jit(solution)/shard_map/ppermute | solution.py:19
  218.1 6.4 %fusion = bf16[1152,1152]{0,1:T(8,128)(2,1)} fusion(bf16[1024,1152]{1,0:T(8,128)(2,1)} %collective-permute-done.1, bf16[1024,1152]{1,0:T(8,128)(2,1)S(1)} %bitcast.30), kind=kOutput, calls=%fused_computation.4 | convolution fusion | flops 2719236096 | bytes 7372800 | tf_op jit(solution)/shard_map/rj,rk->jk/dot_general | solution.py:84
  224.5 5.2 %copy.19 = bf16[1152,1152]{1,0:T(8,128)(2,1)} copy(bf16[1152,1152]{0,1:T(8,128)(2,1)} %fusion) | data formatting | bytes 5308416 | tf_op jit(solution)/shard_map/convert_element_type | solution.py:114
  229.8 3.6 reshape_reshape.6
  233.4 8.3 %pad_maximum_fusion = bf16[16,248832]{1,0:T(8,128)(2,1)} fusion(bf16[16,165888]{1,0:T(8,128)(2,1)} %reshape_reshape.7, bf16[16,82944]{1,0:T(8,128)(2,1)} %reshape_reshape.6), kind=kLoop, calls=%fused_computation.1 | loop fusion | flops 15925248 | bytes 15925248 | tf_op jit(solution)/shard_map/concatenate | solution.py:30
  241.7 7.6 %reshape.82 = bf16[31104,128]{1,0:T(8,128)(2,1)} reshape(bf16[16,248832]{1,0:T(8,128)(2,1)} %pad_maximum_fusion) | data formatting | bytes 15925248 | tf_op jit(solution)/shard_map/reshape | solution.py:32
  249.3 0.0 copy-start.5
  249.3 0.0 all-reduce.3.cloned.1.call-update
  249.3 0.6 copy-done.5
  250.0 0.6 dynamic-slice
  251.2 0.0 copy-start.2
  251.2 7.4 %convolution_convert_fusion.3 = bf16[1024,1152]{1,0:T(8,128)(2,1)} fusion(bf16[1024,1152]{1,0:T(8,128)(2,1)} %collective-permute-done.1, bf16[1,1152,1152]{2,1,0:T(8,128)(2,1)} %all-gather.3.cloned.1.call-done), kind=kOutput, calls=%fused_computation.18 | convolution fusion | flops 2719088640 | bytes 7372800 | tf_op jit(solution)/shard_map/rk,jk->rj/dot_general | solution.py:81
  258.7 0.0 copy-start.1
  258.7 151.7 %all-reduce.3.cloned.1.call-done = bf16[31104,128]{1,0:T(8,128)(2,1)} async-done(((bf16[31104,128]{1,0:T(8,128)(2,1)}), bf16[31104,128]{1,0:T(8,128)(2,1)}) %all-reduce.3.cloned.1.call-update) | async-done | bytes 7962640
  410.3 1.7 dynamic-slice_convert_fusion.1
  412.0 1.8 reshape.84
  413.8 1.9 dynamic-slice_convert_fusion
  415.6 2.1 reshape.85
  417.7 0.0 copy-done.2
  417.7 2.3 multiply_subtract_fusion.1
  419.9 0.0 copy-done.1
  419.9 3.0 multiply_subtract_fusion
Async XLA Ops:
  7.2 56.6 %copy-start = (bf16[1,2,512,1152]{3,2,1,0:T(8,128)(2,1)S(1)}, bf16[1,2,512,1152]{3,2,1,0:T(8,128)(2,1)}, u32[]{:S(2)}) copy-start(bf16[1,2,512,1152]{3,2,1,0:T(8,128)(2,1)} %param.9) | copy-start | bytes 7077892
  7.2 56.6 %all-gather.3.cloned.1.call-start = ((), (), s32[]{:S(2)}) async-start(), calls=%async_computation | async-start | bytes 2820096 | tf_op jit(solution)/shard_map/all_gather | solution.py:91
  9.1 133.1 %all-gather.5.cloned.1.call-start = ((), (), s32[]{:S(2)}) async-start(), calls=%async_computation.1 | async-start | bytes 5640192 | tf_op jit(solution)/shard_map/all_gather | solution.py:92
  11.0 399.3 %all-reduce.3.cloned.1.call-start = ((), (), s32[]{:S(2)}) async-start(), calls=%async_computation.2 | async-start | bytes 15925248
  69.2 71.3 %collective-permute-start = (bf16[1024,1152]{1,0:T(8,128)(2,1)S(1)}, bf16[1024,1152]{1,0:T(8,128)(2,1)}, u32[]{:S(2)}, u32[]{:S(2)}) collective-permute-start(bf16[1024,1152]{1,0:T(8,128)(2,1)S(1)} %convolution_convert_fusion.4), channel_id=1, source_target_pairs={{0,64},{16,80},{32,96},{48,112},{64,0},{80,16},{96,32},{112,48},{1... | collective-permute-start | bytes 7077896 | tf_op jit(solution)/shard_map/ppermute | solution.py:19
  142.1 13.2 %copy-start.3 = (bf16[1,2304,1152]{2,1,0:T(8,128)(2,1)S(1)}, bf16[1,2304,1152]{2,1,0:T(8,128)(2,1)}, u32[]{:S(2)}) copy-start(bf16[1,2304,1152]{2,1,0:T(8,128)(2,1)} %all-gather.5.cloned.1.call-done) | copy-start | bytes 15925252
  161.9 3.2 copy-start.4
  164.4 53.7 %collective-permute-start.1 = (bf16[1024,1152]{1,0:T(8,128)(2,1)}, bf16[1024,1152]{1,0:T(8,128)(2,1)}, u32[]{:S(2)}, u32[]{:S(2)}) collective-permute-start(bf16[1024,1152]{1,0:T(8,128)(2,1)} %get-tuple-element.16), channel_id=1, source_target_pairs={{0,64},{16,80},{32,96},{48,112},{64,0},{80,16},{96,32},{112,48},{1... | collective-permute-start | bytes 7077896 | tf_op jit(solution)/shard_map/ppermute | solution.py:19
  249.3 0.7 copy-start.5
  251.2 166.5 %copy-start.2 = (f32[1,72,1152]{2,1,0:T(8,128)S(1)}, f32[1,72,1152]{2,1,0:T(8,128)}, u32[]{:S(2)}) copy-start(f32[1,72,1152]{2,1,0:T(8,128)} %param.12) | copy-start | bytes 995332
  258.7 161.3 %copy-start.1 = (f32[1,144,1152]{2,1,0:T(8,128)S(1)}, f32[1,144,1152]{2,1,0:T(8,128)}, u32[]{:S(2)}) copy-start(f32[1,144,1152]{2,1,0:T(8,128)} %param.13) | copy-start | bytes 1990660
Sparse Core Ops, SparseCore 0:
  11.0 52.6 all-gather.2
  66.7 75.4 all-gather.4
  249.5 160.8 all-reduce.2
where the time goes:
time: 430 us
  waiting for transfers between devices  316 us (73%)
  matrix products  47.4 us (11%)
  local copies, waits for them, and re-layouts  29.8 us (7%)
  other arithmetic  20.8 us (5%)
  between operations  14.5 us (3%)
    unnamed x4, waiting for transfers between devices  152 us
    ppermute x2, waiting for transfers between devices, swapped(): return lax.ppermute(value, axis, pairs)  110 us
    all_gather x1, waiting for transfers between devices, body(): lax.all_gather(w_proj.astype(jnp.bfloat16), 'dp', axis=1, tiled=True)  52.7 us
    dot_general x1, matrix products, layer_pass(): preact = jnp.dot(joined, skip_full, preferred_element_type=jnp.float32)  13.2 us
    another operation x2, local copies, waits for them, and re-layouts, one_scatter(): lines = jnp.concatenate([b.reshape(count, -1) for b in pieces], axis=1)  9.3 us
  transfers between devices with their start and end apart: 5, of which 5 were waited for; matrix products, arithmetic and copies ran while one was open for 7% of the time, Pallas kernels for 0%

commit v1 on v0

v1 whole, which is shorter than its diff:
```python
import jax
import jax.numpy as jnp
from jax import lax
from jax.sharding import PartitionSpec as P

half_root = 0.7071067811865476
gauss_norm = 0.3989422804014327
beta_one = 0.9
beta_two = 0.95
learn_rate = 0.002
adam_eps = 1e-08
correct_one = 1.0 - 0.9**10
correct_two = 1.0 - 0.95**10


def swapped(value, axis, bit):
    mask = 2**bit
    pairs = [(source, source ^ mask) for source in range(lax.axis_size(axis))]
    return lax.ppermute(value, axis, pairs)


def gelu_parts(preact):
    normal_cdf = 0.5 * (1.0 + lax.erf(preact * half_root))
    density = jnp.exp(-0.5 * preact * preact) * gauss_norm
    return (preact * normal_cdf, normal_cdf + preact * density)


def adam_update(weight, moment, second, grad):
    new_moment = beta_one * moment + (1.0 - beta_one) * grad
    new_second = beta_two * second + (1.0 - beta_two) * grad * grad
    step_size = new_moment / correct_one / (jnp.sqrt(new_second / correct_two) + adam_eps)
    return (weight - learn_rate * step_size, new_moment, new_second)


def swap_partner(value):
    bit = lax.axis_size("section").bit_length() - 2
    return swapped(value, "section", bit)


def body(enc_in, dec_in, cotangent, w_proj, w_skip, m_proj, v_proj, m_skip, v_skip):
    micro, tokens_here, width = enc_in.shape[1:]
    rows = micro * tokens_here
    enc_rows = swap_partner(enc_in[0].reshape(rows, width))
    proj_shard = swap_partner(w_proj[0].astype(jnp.bfloat16))
    proj_full = lax.all_gather(proj_shard, "dp", axis=0, tiled=True)
    skip_full = lax.all_gather(w_skip[0].astype(jnp.bfloat16), "dp", axis=0, tiled=True)
    dec_rows = dec_in[0].reshape(rows, width)
    out_grad = cotangent[0].reshape(rows, width)
    skip = jnp.dot(enc_rows, proj_full, preferred_element_type=jnp.float32).astype(jnp.bfloat16)
    preact = jnp.dot(dec_rows, skip_full[:width], preferred_element_type=jnp.float32) + jnp.dot(
        skip, skip_full[width:], preferred_element_type=jnp.float32
    )
    activated, gelu_slope = gelu_parts(preact)
    dec_out = activated.astype(jnp.bfloat16)
    pre_grad = (out_grad.astype(jnp.float32) * gelu_slope).astype(jnp.bfloat16)
    skip_grad = jnp.einsum(
        "rk,jk->rj", pre_grad, skip_full[width:], preferred_element_type=jnp.float32
    ).astype(jnp.bfloat16)
    enc_grad = swap_partner(
        jnp.einsum("rk,jk->rj", skip_grad, proj_full, preferred_element_type=jnp.float32).astype(
            jnp.bfloat16
        )
    )
    dec_grad = jnp.einsum(
        "rk,jk->rj", pre_grad, skip_full[:width], preferred_element_type=jnp.float32
    ).astype(jnp.bfloat16)
    grad_dec = jnp.einsum("rj,rk->jk", dec_rows, pre_grad, preferred_element_type=jnp.float32)
    grad_mid = jnp.einsum("rj,rk->jk", skip, pre_grad, preferred_element_type=jnp.float32)
    grad_skip = jnp.concatenate([grad_dec, grad_mid], axis=0).astype(jnp.bfloat16)
    grad_proj = jnp.einsum(
        "rj,rk->jk", enc_rows, skip_grad, preferred_element_type=jnp.float32
    ).astype(jnp.bfloat16)
    count = lax.axis_size("dp")
    grads = jnp.concatenate(
        [
            grad_skip.reshape(count, -1, width),
            jnp.pad(grad_proj.reshape(count, -1, width), ((0, 0), (0, 8), (0, 0))),
        ],
        axis=1,
    )
    shard = lax.psum_scatter(grads, "dp", scatter_dimension=0, tiled=True)[0]
    proj_sum = swap_partner(shard[w_skip.shape[1] :][: w_proj.shape[1]])
    skip_sum = shard[: w_skip.shape[1]]
    new_w_proj, new_m_proj, new_v_proj = adam_update(
        w_proj[0], m_proj[0], v_proj[0], proj_sum.astype(jnp.float32)
    )
    new_w_skip, new_m_skip, new_v_skip = adam_update(
        w_skip[0], m_skip[0], v_skip[0], skip_sum.astype(jnp.float32)
    )
    shape = (1, micro, tokens_here, width)
    return (
        dec_out.reshape(shape),
        enc_grad.reshape(shape),
        dec_grad.reshape(shape),
        new_w_proj[None],
        new_m_proj[None],
        new_v_proj[None],
        new_w_skip[None],
        new_m_skip[None],
        new_v_skip[None],
    )


def solution(mesh):
    in_specs = (
        P("section", None, "dp", None),
        P("section", None, "dp", None),
        P("section", None, "dp", None),
        P("section", "dp", None),
        P("section", "dp", None),
        P("section", "dp", None),
        P("section", "dp", None),
        P("section", "dp", None),
        P("section", "dp", None),
    )
    out_specs = (
        P("section", None, "dp", None),
        P("section", None, "dp", None),
        P("section", None, "dp", None),
        P("section", "dp", None),
        P("section", "dp", None),
        P("section", "dp", None),
        P("section", "dp", None),
        P("section", "dp", None),
        P("section", "dp", None),
    )
    return jax.shard_map(body, mesh=mesh, in_specs=in_specs, out_specs=out_specs, check_vma=False)
```

time: 430 us -> 306 us (0.71)
  waiting for transfers between devices: 316 us -> 221 us
  local copies, waits for them, and re-layouts: 29.8 us -> 7.81 us
  other arithmetic: 20.8 us -> 10.8 us
    unnamed x4 -> x3, waiting for transfers between devices: 152 us -> 0.05 us
    reduce_scatter x0 -> x1, waiting for transfers between devices: none -> 40.7 us  [body(): shard = lax.psum_scatter(grads, 'dp', scatter_dimension=0, tiled=True)[0]]
    ppermute x2 -> x4, waiting for transfers between devices: 110 us -> 128 us  [swapped(): return lax.ppermute(value, axis, pairs)]
    another operation x2 -> x0, local copies, waits for them, and re-layouts: 9.3 us -> none  [one_scatter(): lines = jnp.concatenate([b.reshape(count, -1) for b in pieces], axis=1)]
    convert_element_type x3 -> x0, local copies, waits for them, and re-layouts: 9.05 us -> none  [the longest x1 5.23 us: body(): result[3].astype(jnp.bfloat16)]
    reshape x1 -> x0, local copies, waits for them, and re-layouts: 7.62 us -> none  [one_scatter(): jnp.pad(lines, ((0, 0), (0, span * 128 - lines.shape[1]))).reshape(-1, 128)]
    unnamed x13 -> x39, local copies, waits for them, and re-layouts: 1.24 us -> 6.88 us
    dot_general x6 -> x9, matrix products: 47.4 us -> 47.2 us  [the longest x1 7.52 us: body(): jnp.dot(skip, skip_full[width:], preferred_element_type=jnp.float32)]
  transfers between devices with their start and end apart: 5 -> 7, of which waited for: 5 -> 6; matrix products, arithmetic and copies ran while one was open for 7% -> 7% of each run, Pallas kernels for 0% -> 0%
where the time goes in v1:
time: 306 us
  waiting for transfers between devices  221 us (72%)
  matrix products  47.2 us (15%)
  between operations  13.9 us (5%)
  other arithmetic  10.8 us (4%)
  local copies, waits for them, and re-layouts  7.81 us (3%)
  starting transfers between devices  5.49 us (2%)
    ppermute x4, waiting for transfers between devices, swapped(): return lax.ppermute(value, axis, pairs)  128 us
    all_gather x1, waiting for transfers between devices, body(): lax.all_gather(w_skip[0].astype(jnp.bfloat16), 'dp', axis=0, tiled=True)  52 us
    reduce_scatter x1, waiting for transfers between devices, body(): shard = lax.psum_scatter(grads, 'dp', scatter_dimension=0, tiled=True)[0]  40.7 us
    dot_general x1, matrix products, body(): jnp.dot(skip, skip_full[width:], preferred_element_type=jnp.float32)  7.52 us
    dot_general x1, matrix products, body(): jnp.dot(enc_rows, proj_full, preferred_element_type=jnp.float32)  7.36 us
    unnamed x39, local copies, waits for them, and re-layouts  6.88 us
  transfers between devices with their start and end apart: 7, of which 6 were waited for; matrix products, arithmetic and copies ran while one was open for 7% of the time, Pallas kernels for 0%

profile of v1, /device:TPU:0, one launch (start us, length us, event | category | flops | bytes accessed | tf_op | source)
XLA Modules:
  0.0 305.9 jit_solution(2849526476837761508)
XLA Ops:
  7.2 0.0 copy-start
  7.2 0.0 all-gather.4.cloned.1.call-start
  7.2 1.1 bitcast_convert_fusion
  8.4 2.1 collective-permute-start.1
  10.5 4.2 %collective-permute-done.1 = bf16[72,1152]{1,0:T(8,128)(2,1)S(1)} collective-permute-done((bf16[72,1152]{1,0:T(8,128)(2,1)S(1)}, bf16[72,1152]{1,0:T(8,128)(2,1)S(1)}, u32[]{:S(2)}, u32[]{:S(2)}) %collective-permute-start.1) | collective-permute-done | bytes 165920 | tf_op jit(solution)/shard_map/ppermute | solution.py:19
  14.7 0.0 copy-start.8
  14.7 0.7 copy-done.8
  15.4 0.0 all-gather.4.cloned.1.call-update
  15.4 0.0 all-gather.6.cloned.1.call-start
  15.5 1.9 convert_element_type.55
  17.3 0.0 all-gather.6.cloned.1.call-update
  17.4 0.0 reduce-scatter.2.cloned.1.call-start
  17.4 1.8 collective-permute-start
  19.2 59.9 %collective-permute-done = bf16[1024,1152]{1,0:T(8,128)(2,1)} collective-permute-done((bf16[1024,1152]{1,0:T(8,128)(2,1)}, bf16[1024,1152]{1,0:T(8,128)(2,1)}, u32[]{:S(2)}, u32[]{:S(2)}) %collective-permute-start) | collective-permute-done | bytes 2359328 | tf_op jit(solution)/shard_map/ppermute | solution.py:19
  79.1 7.4 %convolution_convert_fusion.6 = bf16[1024,1152]{1,0:T(8,128)(2,1)} fusion(bf16[1024,1152]{1,0:T(8,128)(2,1)} %collective-permute-done, bf16[1152,1152]{1,0:T(8,128)(2,1)} %all-gather.4.cloned.1.call-done), kind=kOutput, calls=%fused_computation.21 | convolution fusion | flops 2719088640 | bytes 7372800 | tf_op jit(solution)/shard_map/dot_general | solution.py:49
  86.5 52.0 %all-gather.6.cloned.1.call-done = bf16[1,2304,1152]{2,1,0:T(8,128)(2,1)} async-done(((bf16[1,144,1152]{2,1,0:T(8,128)(2,1)}), bf16[1,2304,1152]{2,1,0:T(8,128)(2,1)}) %all-gather.6.cloned.1.call-update) | async-done | bytes 5308432 | tf_op jit(solution)/shard_map/all_gather | solution.py:46
  138.5 0.0 copy-done
  138.5 0.0 copy-start.9
  138.5 0.0 copy-start.10
  138.5 0.0 copy-start.14
  138.5 5.4 %fusion.9 = f32[1024,1152]{1,0:T(8,128)S(1)} fusion(bf16[1024,1152]{1,0:T(8,128)(2,1)S(1)} %bitcast.63, bf16[1,2304,1152]{2,1,0:T(8,128)(2,1)} %all-gather.6.cloned.1.call-done), kind=kOutput, calls=%fused_computation.24 | convolution fusion | flops 2717908992 | bytes 9732096 | tf_op jit(solution)/shard_map/dot_general | solution.py:50
  143.9 0.0 copy-done.9
  143.9 0.0 copy-done.10
  143.9 0.0 copy-done.14
  143.9 7.5 %fusion.8 = (bf16[1024,1152]{1,0:T(8,128)(2,1)S(1)}, bf16[1024,1152]{1,0:T(8,128)(2,1)}) fusion(bf16[1,2,512,1152]{3,2,1,0:T(8,128)(2,1)S(1)} %copy-done.10, f32[1024,1152]{1,0:T(8,128)S(1)} %fusion.9, bf16[1024,1152]{1,0:T(8,128)(2,1)S(1)} %copy-done.14, bf16[1,2304,1152]{2,1,0:T(8,128)(2,1)S(1)} %copy-done.9), kind=kOutput, calls=%fused_computation.14 | convolution fusion | flops 2734424064 | bytes 16809984 | tf_op jit(solution)/shard_map/dot_general | solution.py:50
  151.5 0.0 copy-start.11
  151.5 3.3 %convolution_convert_fusion.1 = bf16[1152,1152]{1,0:T(8,128)(2,1)S(1)} fusion(bf16[1024,1152]{1,0:T(8,128)(2,1)S(1)} %copy-done.14, bf16[1024,1152]{1,0:T(8,128)(2,1)S(1)} %get-tuple-element.12), kind=kOutput, calls=%fused_computation.4 | convolution fusion | flops 2719236096 | bytes 7372800 | tf_op jit(solution)/shard_map/rj,rk->jk/dot_general | solution.py:68
  154.8 0.0 copy-done.11
  154.8 3.3 %fusion.2 = bf16[1152,1152]{1,0:T(8,128)(2,1)S(1)} fusion(bf16[1024,1152]{1,0:T(8,128)(2,1)S(1)} %get-tuple-element.12, bf16[1024,1152]{1,0:T(8,128)(2,1)S(1)} %bitcast.64), kind=kOutput, calls=%fused_computation.7 | convolution fusion | flops 2719236096 | bytes 7372800 | tf_op jit(solution)/shard_map/rj,rk->jk/dot_general | solution.py:67
  158.2 0.0 copy-start.12
  158.2 0.4 pad_maximum_fusion
  158.6 1.2 copy-done.12
  159.8 4.0 %convolution_convert_fusion.5 = bf16[1024,1152]{1,0:T(8,128)(2,1)S(1)} fusion(bf16[1024,1152]{1,0:T(8,128)(2,1)S(1)} %copy-done.12, bf16[1,2304,1152]{2,1,0:T(8,128)(2,1)S(1)} %copy-done.9), kind=kOutput, calls=%fused_computation.20 | convolution fusion | flops 2719088640 | bytes 7372800 | tf_op jit(solution)/shard_map/rk,jk->rj/dot_general | solution.py:56
  163.8 0.0 copy-start.15
  163.9 5.8 %convolution_convert_fusion = bf16[1152,1152]{0,1:T(8,128)(2,1)S(1)} fusion(bf16[1024,1152]{1,0:T(8,128)(2,1)S(1)} %convolution_convert_fusion.5, bf16[1024,1152]{1,0:T(8,128)(2,1)} %collective-permute-done), kind=kOutput, calls=%fused_computation.3 | convolution fusion | flops 2719236096 | bytes 7372800 | tf_op jit(solution)/shard_map/rj,rk->jk/dot_general | solution.py:70
  169.6 0.0 copy-done.15
  169.7 3.7 %fusion.1 = bf16[16,224,1152]{2,1,0:T(8,128)(2,1)} fusion(bf16[16,72,1152]{2,1,0:T(8,128)(2,1)S(1)} %bitcast.66, bf16[16,144,1152]{2,1,0:T(8,128)(2,1)S(1)} %bitcast.65), kind=kLoop, calls=%fused_computation.2 | loop fusion | flops 24772608 | bytes 16220160 | tf_op jit(solution)/shard_map/concatenate | solution.py:74
  173.4 0.0 reduce-scatter.2.cloned.1.call-update
  173.4 1.6 copy-done.16
  175.0 5.6 %convolution_convert_fusion.4 = bf16[1024,1152]{1,0:T(8,128)(2,1)S(1)} fusion(bf16[1024,1152]{1,0:T(8,128)(2,1)S(1)} %copy-done.16, bf16[1152,1152]{1,0:T(8,128)(2,1)} %all-gather.4.cloned.1.call-done), kind=kOutput, calls=%fused_computation.19 | convolution fusion | flops 2719088640 | bytes 7372800 | tf_op jit(solution)/shard_map/rk,jk->rj/dot_general | solution.py:60
  180.7 0.0 copy-start.2
  180.7 0.0 copy-start.4
  180.7 0.0 copy-start.5
  180.7 0.8 collective-permute-start.2
  181.4 0.0 slice-done
  181.5 0.0 slice-done.1
  181.5 0.0 copy-done.13
  181.5 4.8 %convolution_convert_fusion.3 = bf16[1024,1152]{1,0:T(8,128)(2,1)} fusion(bf16[1024,1152]{1,0:T(8,128)(2,1)S(1)} %copy-done.13, bf16[1,2304,1152]{2,1,0:T(8,128)(2,1)S(1)} %bitcast.68), kind=kOutput, calls=%fused_computation.18 | convolution fusion | flops 2719088640 | bytes 7372800 | tf_op jit(solution)/shard_map/rk,jk->rj/dot_general | solution.py:64
  186.2 61.6 %collective-permute-done.2 = bf16[1024,1152]{1,0:T(8,128)(2,1)} collective-permute-done((bf16[1024,1152]{1,0:T(8,128)(2,1)S(1)}, bf16[1024,1152]{1,0:T(8,128)(2,1)}, u32[]{:S(2)}, u32[]{:S(2)}) %collective-permute-start.2) | collective-permute-done | bytes 2359328 | tf_op jit(solution)/shard_map/ppermute | solution.py:19
  247.9 40.7 %reduce-scatter.2.cloned.1.call-done = bf16[1,224,1152]{2,1,0:T(8,128)(2,1)} async-done(((bf16[16,224,1152]{2,1,0:T(8,128)(2,1)}), bf16[1,224,1152]{2,1,0:T(8,128)(2,1)}) %reduce-scatter.2.cloned.1.call-update) | async-done | bytes 516112 | tf_op jit(solution)/shard_map/reduce_scatter | solution.py:81
  288.5 0.9 slice_bitcast_fusion.6
  289.4 0.7 collective-permute-start.3
  290.1 0.0 copy-done.2
  290.1 0.0 copy-done.4
  290.1 0.0 copy-done.5
  290.1 2.5 multiply_subtract_fusion
  292.7 2.2 collective-permute-done.3
  294.9 0.0 copy-done.3
  294.9 0.0 copy-done.6
  294.9 0.0 copy-done.7
  294.9 0.0 copy-start.1
  294.9 1.2 fusion.16
  296.1 3.2 %copy.19 = bf16[1,2,512,1152]{3,2,1,0:T(8,128)(2,1)} copy(bf16[1,2,512,1152]{3,2,1,0:T(8,128)(2,1)} %bitcast.7) | data formatting | bytes 4718592
  299.3 0.0 copy-done.1
  (9 shorter events, 0.0 us)
Async XLA Ops:
  7.2 131.3 %copy-start = (bf16[1,2,512,1152]{3,2,1,0:T(8,128)(2,1)S(1)}, bf16[1,2,512,1152]{3,2,1,0:T(8,128)(2,1)}, u32[]{:S(2)}) copy-start(bf16[1,2,512,1152]{3,2,1,0:T(8,128)(2,1)} %param.10) | copy-start | bytes 7077892
  7.2 71.9 %all-gather.4.cloned.1.call-start = ((), (), s32[]{:S(2)}) async-start(), calls=%async_computation.1 | async-start | bytes 2820096 | tf_op jit(solution)/shard_map/all_gather | solution.py:45
  8.4 6.4 %collective-permute-start.1 = (bf16[72,1152]{1,0:T(8,128)(2,1)S(1)}, bf16[72,1152]{1,0:T(8,128)(2,1)S(1)}, u32[]{:S(2)}, u32[]{:S(2)}) collective-permute-start(bf16[72,1152]{1,0:T(8,128)(2,1)S(1)} %bitcast_convert_fusion), channel_id=1, source_target_pairs={{0,64},{16,80},{32,96},{48,112},{64,0},{80,16},{96,32},{112,48},{1... | collective-permute-start | bytes 497672 | tf_op jit(solution)/shard_map/ppermute | solution.py:19
  14.7 0.7 copy-start.8
  15.4 123.1 %all-gather.6.cloned.1.call-start = ((), (), s32[]{:S(2)}) async-start(), calls=%async_computation.3 | async-start | bytes 5640192 | tf_op jit(solution)/shard_map/all_gather | solution.py:46
  17.4 271.2 %reduce-scatter.2.cloned.1.call-start = ((), (), s32[]{:S(2)}) async-start(), calls=%async_computation.2 | async-start | bytes 8773632 | tf_op jit(solution)/shard_map/reduce_scatter | solution.py:81
  17.4 61.7 %collective-permute-start = (bf16[1024,1152]{1,0:T(8,128)(2,1)}, bf16[1024,1152]{1,0:T(8,128)(2,1)}, u32[]{:S(2)}, u32[]{:S(2)}) collective-permute-start(bf16[1024,1152]{1,0:T(8,128)(2,1)} %bitcast.69), channel_id=1, source_target_pairs={{0,64},{16,80},{32,96},{48,112},{64,0},{80,16},{96,32},{112,48},{1... | collective-permute-start | bytes 7077896 | tf_op jit(solution)/shard_map/ppermute | solution.py:19
  138.5 5.4 %copy-start.9 = (bf16[1,2304,1152]{2,1,0:T(8,128)(2,1)S(1)}, bf16[1,2304,1152]{2,1,0:T(8,128)(2,1)}, u32[]{:S(2)}) copy-start(bf16[1,2304,1152]{2,1,0:T(8,128)(2,1)} %all-gather.6.cloned.1.call-done) | copy-start | bytes 15925252
  138.5 5.4 %copy-start.10 = (bf16[1,2,512,1152]{3,2,1,0:T(8,128)(2,1)S(1)}, bf16[1,2,512,1152]{3,2,1,0:T(8,128)(2,1)}, u32[]{:S(2)}) copy-start(bf16[1,2,512,1152]{3,2,1,0:T(8,128)(2,1)} %param.11) | copy-start | bytes 7077892
  138.5 5.4 %copy-start.14 = (bf16[1024,1152]{1,0:T(8,128)(2,1)S(1)}, bf16[1024,1152]{1,0:T(8,128)(2,1)}, u32[]{:S(2)}) copy-start(bf16[1024,1152]{1,0:T(8,128)(2,1)} %convolution_convert_fusion.6) | copy-start | bytes 7077892
  151.5 3.3 %copy-start.11 = (bf16[1024,1152]{1,0:T(8,128)(2,1)}, bf16[1024,1152]{1,0:T(8,128)(2,1)S(1)}, u32[]{:S(2)}) copy-start(bf16[1024,1152]{1,0:T(8,128)(2,1)S(1)} %get-tuple-element.12) | copy-start | bytes 7077892
  158.2 1.7 copy-start.12
  163.8 5.8 %copy-start.15 = (bf16[1024,1152]{1,0:T(8,128)(2,1)}, bf16[1024,1152]{1,0:T(8,128)(2,1)S(1)}, u32[]{:S(2)}) copy-start(bf16[1024,1152]{1,0:T(8,128)(2,1)S(1)} %convolution_convert_fusion.5) | copy-start | bytes 7077892
  173.3 1.7 copy-start.16
  173.3 8.1 %slice-start = ((s8[5308416]{0:T(1024)(128)(4,1)}), s8[1114112]{0:T(1024)(128)(4,1)S(1)}, s32[]{:S(2)}) async-start(s8[5308416]{0:T(1024)(128)(4,1)} %bitcast.67), calls=%async_computation.4 | async-start | bytes 2228224
  175.0 6.4 %slice-start.1 = ((s8[5308416]{0:T(1024)(128)(4,1)}), s8[4194304]{0:T(1024)(128)(4,1)S(1)}, s32[]{:S(2)}) async-start(s8[5308416]{0:T(1024)(128)(4,1)} %bitcast.67), calls=%async_computation.5 | async-start | bytes 8388608
  175.0 6.4 %copy-start.13 = (bf16[1024,1152]{1,0:T(8,128)(2,1)S(1)}, bf16[1024,1152]{1,0:T(8,128)(2,1)}, u32[]{:S(2)}) copy-start(bf16[1024,1152]{1,0:T(8,128)(2,1)} %copy-done.11) | copy-start | bytes 7077892
  180.7 109.5 %copy-start.2 = (f32[1,144,1152]{2,1,0:T(8,128)S(1)}, f32[1,144,1152]{2,1,0:T(8,128)}, u32[]{:S(2)}) copy-start(f32[1,144,1152]{2,1,0:T(8,128)} %param.13) | copy-start | bytes 1990660
  180.7 109.5 %copy-start.4 = (f32[1,144,1152]{2,1,0:T(8,128)S(1)}, f32[1,144,1152]{2,1,0:T(8,128)}, u32[]{:S(2)}) copy-start(f32[1,144,1152]{2,1,0:T(8,128)} %param.16) | copy-start | bytes 1990660
  180.7 109.5 %copy-start.5 = (f32[1,144,1152]{2,1,0:T(8,128)S(1)}, f32[1,144,1152]{2,1,0:T(8,128)}, u32[]{:S(2)}) copy-start(f32[1,144,1152]{2,1,0:T(8,128)} %param.17) | copy-start | bytes 1990660
  180.7 67.2 %collective-permute-start.2 = (bf16[1024,1152]{1,0:T(8,128)(2,1)S(1)}, bf16[1024,1152]{1,0:T(8,128)(2,1)}, u32[]{:S(2)}, u32[]{:S(2)}) collective-permute-start(bf16[1024,1152]{1,0:T(8,128)(2,1)S(1)} %convolution_convert_fusion.4), channel_id=1, source_target_pairs={{0,64},{16,80},{32,96},{48,112},{64,0},{80,16},{96,32},{112,48},{1... | collective-permute-start | bytes 7077896 | tf_op jit(solution)/shard_map/ppermute | solution.py:19
  186.2 108.6 %copy-start.3 = (f32[1,72,1152]{2,1,0:T(8,128)S(1)}, f32[1,72,1152]{2,1,0:T(8,128)}, u32[]{:S(2)}) copy-start(f32[1,72,1152]{2,1,0:T(8,128)} %param.12) | copy-start | bytes 995332
  186.2 108.6 %copy-start.6 = (f32[1,72,1152]{2,1,0:T(8,128)S(1)}, f32[1,72,1152]{2,1,0:T(8,128)}, u32[]{:S(2)}) copy-start(f32[1,72,1152]{2,1,0:T(8,128)} %param.15) | copy-start | bytes 995332
  186.2 108.6 %copy-start.7 = (f32[1,72,1152]{2,1,0:T(8,128)S(1)}, f32[1,72,1152]{2,1,0:T(8,128)}, u32[]{:S(2)}) copy-start(f32[1,72,1152]{2,1,0:T(8,128)} %param.14) | copy-start | bytes 995332
  289.4 5.4 %collective-permute-start.3 = (bf16[72,1152]{1,0:T(8,128)(2,1)S(1)}, bf16[72,1152]{1,0:T(8,128)(2,1)S(1)}, u32[]{:S(2)}, u32[]{:S(2)}) collective-permute-start(bf16[72,1152]{1,0:T(8,128)(2,1)S(1)} %slice_bitcast_fusion.6), channel_id=1, source_target_pairs={{0,64},{16,80},{32,96},{48,112},{64,0},{80,16},{96,32},{112,48},{1... | collective-permute-start | bytes 497672 | tf_op jit(solution)/shard_map/ppermute | solution.py:19
  294.9 4.5 %copy-start.1 = (bf16[1,2,512,1152]{3,2,1,0:T(8,128)(2,1)S(1)}, bf16[1,2,512,1152]{3,2,1,0:T(8,128)(2,1)}, u32[]{:S(2)}) copy-start(bf16[1,2,512,1152]{3,2,1,0:T(8,128)(2,1)} %param.10) | copy-start | bytes 7077892
Sparse Core Ops, SparseCore 0:
  15.6 61.1 all-gather.3
  79.6 58.8 all-gather.5
  173.5 114.9 reduce-scatter.1
